TPU v7x, 256 devices: a whole 4x4x8 slice. The times are simulated.
256 devices in a mesh: zonal: 64 (over y_lo, x, z), merid: 4 (over y_hi, core).
Axes of the slice: x: 4, y: 4 (y_hi: 2, y_lo: 2; y = y_hi * 2 + y_lo), z: 8, core: 2. Of those that a mesh axis runs over, the one named last changes fastest.
Arguments:
- field: bfloat16 [64, 4096, 256], P('merid', 'zonal'), may hold values from -6 to 6
- weight_one: bfloat16 [3, 3, 256, 256], replicated, may hold values from -0.125 to 0.125
- bias_one: float32 [256], replicated, may hold values from -3 to 3
- weight_two: bfloat16 [3, 3, 256, 256], replicated, may hold values from -0.125 to 0.125
- bias_two: float32 [256], replicated, may hold values from -3 to 3
- depth_levels: int32 [64, 4096], P('merid', 'zonal'), may hold values from 0 to 64
- fold_partner: int32 [4096], replicated, may hold values from 0 to 4095, as said below
- cotangent: bfloat16 [64, 4096, 256], P('merid', 'zonal'), may hold values from -6 to 6
Outputs:
- output: bfloat16 [64, 4096, 256], P('merid', 'zonal')
- input_grad: bfloat16 [64, 4096, 256], P('merid', 'zonal')
- grad_one: float32 [3, 3, 256, 256], replicated
- grad_two: float32 [3, 3, 256, 256], replicated
Inputs may be any that keep to these rules, and one draw needn't show every extreme that they name: fold_partner[i] = (4095 - i + s) mod 4096 with one pivot offset s, 0 to 4095, for the whole table.
All inputs are finite; a program needn't handle non-finite values.
Results may differ from a plain program's by a relative error of at most 0.003.
Values may be sent and summed in bfloat16 or wider, within the bound.
No kernel may reach another device: no remote copies, remote signals or barrier semaphores. Data moves between devices by JAX's collectives and lax.ppermute only.
A program may use at most 128 MiB of HBM per device.

v0:
```python
import math
import jax
import jax.numpy as jnp
from jax import lax
from jax.sharding import PartitionSpec as P

LEV = 64


def with_halo(cells, sides, width, closed):
    for axis, dim in sides:
        count = lax.axis_size(axis)
        ends = count if closed else count - 1
        head = lax.slice_in_dim(cells, 0, width, axis=dim)
        tail = lax.slice_in_dim(cells, cells.shape[dim] - width, cells.shape[dim], axis=dim)
        cells = jnp.concatenate(
            [
                lax.ppermute(tail, axis, [(i, (i + 1) % count) for i in range(ends)]),
                cells,
                lax.ppermute(head, axis, [((i + 1) % count, i) for i in range(ends)]),
            ],
            axis=dim,
        )
    return cells


def level_mask(depth_levels, channels):
    level_index = lax.broadcasted_iota(jnp.int32, (1, 1, channels), 2) % LEV
    return (level_index < depth_levels[:, :, None]).astype(jnp.float32)


def fold_forward(top_row, fold_partner):
    columns = top_row.shape[0]
    whole_row = lax.all_gather(top_row, "zonal", axis=0, tiled=True)
    partners = lax.dynamic_slice_in_dim(fold_partner, lax.axis_index("zonal") * columns, columns, 0)
    return jnp.take(whole_row, partners, axis=0)


def fold_backward(fold_grad, fold_partner):
    columns = fold_grad.shape[0]
    whole_row = lax.all_gather(fold_grad.astype(jnp.bfloat16), "zonal", axis=0, tiled=True).astype(
        fold_grad.dtype
    )
    partners = lax.dynamic_slice_in_dim(fold_partner, lax.axis_index("zonal") * columns, columns, 0)
    return jnp.take(whole_row, partners, axis=0)


def pad_field(values, fold_partner, is_top):
    with_rows = with_halo(values, (("merid", 0),), 1, False)
    fold_row = fold_forward(values[-1], fold_partner)
    upper_row = jnp.where(is_top, fold_row, with_rows[-1])
    with_rows = jnp.concatenate([with_rows[:-1], upper_row[None]], axis=0)
    return with_halo(with_rows, (("zonal", 1),), 1, True)


def unpad_grad(grad_pad, fold_partner, is_top):
    sides = jnp.concatenate([grad_pad[:, :1], grad_pad[:, -1:]], axis=1)
    returned = with_halo(sides.astype(jnp.bfloat16), (("zonal", 1),), 1, True).astype(sides.dtype)
    inner = grad_pad[:, 1:-1]
    inner = inner.at[:, 0].add(returned[:, 0]).at[:, -1].add(returned[:, 3])
    rims = jnp.concatenate([inner[:1], inner[-1:]], axis=0)
    back_rows = with_halo(rims.astype(jnp.bfloat16), (("merid", 0),), 1, False).astype(rims.dtype)
    folded = fold_backward(inner[-1], fold_partner)
    top_added = back_rows[3] + jnp.where(is_top, folded, jnp.zeros_like(folded))
    middle = inner[1:-1]
    return middle.at[0].add(back_rows[0]).at[-1].add(top_added)


def patches_of(padded, rows, columns):
    pieces = [
        padded[row_step : row_step + rows, col_step : col_step + columns]
        for row_step in range(3)
        for col_step in range(3)
    ]
    return jnp.concatenate(pieces, axis=2).reshape(rows * columns, -1)


def transpose_conv(delta, flat_weight, rows, columns):
    channels = delta.shape[1]
    parts = lax.dot_general(
        delta, flat_weight, (((1,), (1,)), ((), ())), preferred_element_type=jnp.float32
    )
    parts = parts.reshape(rows, columns, 9, channels)
    grad_pad = jnp.zeros((rows + 2, columns + 2, channels), jnp.float32)
    for row_step in range(3):
        for col_step in range(3):
            grad_pad = grad_pad.at[row_step : row_step + rows, col_step : col_step + columns].add(
                parts[:, :, 3 * row_step + col_step]
            )
    return grad_pad


def kernel_grad(patches, delta):
    channels = delta.shape[1]
    summed = lax.dot_general(
        patches, delta, (((0,), (0,)), ((), ())), preferred_element_type=jnp.float32
    )
    return summed.reshape(3, 3, channels, channels)


def shards(
    field, weight_one, bias_one, weight_two, bias_two, depth_levels, fold_partner, cotangent
):
    rows, columns, channels = field.shape
    is_top = lax.axis_index("merid") == lax.axis_size("merid") - 1
    mask = level_mask(depth_levels, channels)
    flat_one = weight_one.reshape(9 * channels, channels)
    flat_two = weight_two.reshape(9 * channels, channels)
    patches_one = patches_of(pad_field(field, fold_partner, is_top), rows, columns)
    pre_one = (
        jnp.dot(patches_one, flat_one, preferred_element_type=jnp.float32).reshape(
            rows, columns, channels
        )
        + bias_one
    )
    hidden = (jax.nn.gelu(pre_one) * mask).astype(jnp.bfloat16)
    patches_two = patches_of(pad_field(hidden, fold_partner, is_top), rows, columns)
    pre_two = jnp.dot(patches_two, flat_two, preferred_element_type=jnp.float32).reshape(
        rows, columns, channels
    )
    output = ((field.astype(jnp.float32) + pre_two + bias_two) * mask).astype(jnp.bfloat16)
    masked_grad = cotangent.astype(jnp.float32) * mask
    delta_two = masked_grad.astype(jnp.bfloat16).reshape(rows * columns, channels)
    grad_two = kernel_grad(patches_two, delta_two)
    hidden_grad = unpad_grad(
        transpose_conv(delta_two, flat_two, rows, columns), fold_partner, is_top
    )
    _, gelu_back = jax.vjp(jax.nn.gelu, pre_one)
    delta_one = (
        gelu_back(hidden_grad * mask)[0].astype(jnp.bfloat16).reshape(rows * columns, channels)
    )
    grad_one = kernel_grad(patches_one, delta_one)
    field_grad = unpad_grad(
        transpose_conv(delta_one, flat_one, rows, columns), fold_partner, is_top
    )
    input_grad = (masked_grad + field_grad).astype(jnp.bfloat16)
    grad_one, grad_two = lax.psum((grad_one, grad_two), ("zonal", "merid"))
    scale = 1.0 / math.sqrt(rows * columns * lax.axis_size("zonal") * lax.axis_size("merid"))
    return (output, input_grad, grad_one * scale, grad_two * scale)


def solution(mesh):
    placed = (
        P("merid", "zonal", None),
        P(),
        P(),
        P(),
        P(),
        P("merid", "zonal"),
        P(),
        P("merid", "zonal", None),
    )
    return jax.shard_map(
        shards,
        mesh=mesh,
        in_specs=placed,
        out_specs=(P("merid", "zonal", None), P("merid", "zonal", None), P(), P()),
        check_vma=False,
    )
```

profile of v0, /device:TPU:97, one launch (start us, length us, event | category | flops | bytes accessed | tf_op | source)
XLA Modules:
  0.0 1509.0 jit_solution(12286972379343277605)
XLA Ops:
  19.0 6.4 scatter-add.89
  31.1 6.4 scatter-add.90
  41.3 5.1 scatter-add.94
  48.8 5.1 scatter-add.95
  57.8 5.1 scatter-add.99
  65.3 5.1 scatter-add.100
  83.2 6.8 collective-permute-start
  94.1 5.1 collective-permute-start.10
  101.2 157.8 %all-gather.9.cloned.1.call-done = bf16[1,4096,256]{2,1,0:T(8,128)(2,1)} async-done(((bf16[1,64,256]{2,1,0:T(8,128)(2,1)}), bf16[1,4096,256]{2,1,0:T(8,128)(2,1)}) %all-gather.9.cloned.1.call-update) | async-done | bytes 2097168 | tf_op jit(solution)/shard_map/all_gather | solution.py:34
  276.2 282.4 %all-gather.13.cloned.1.call-done = bf16[1,4096,256]{2,1,0:T(8,128)(2,1)} async-done(((bf16[1,64,256]{2,1,0:T(8,128)(2,1)}), bf16[1,4096,256]{2,1,0:T(8,128)(2,1)}) %all-gather.13.cloned.1.call-update) | async-done | bytes 2097168 | tf_op jit(solution)/shard_map/all_gather | solution.py:41
  565.4 5.2 fusion.8
  579.7 6.4 scatter-add.110
  619.2 50.8 %collective-permute-start.5 = (bf16[1,64,256]{2,1,0:T(8,128)(2,1)}, bf16[1,64,256]{2,1,0:T(8,128)(2,1)S(1)}, u32[]{:S(2)}, u32[]{:S(2)}) collective-permute-start(bf16[1,64,256]{2,1,0:T(8,128)(2,1)} %get-tuple-element.341), channel_id=1, source_target_pairs={{1,0},{2,1},{3,2},{5,4},{6,5},{7,6},{9,8},{10,9},{11,10},{13,12},{... | collective-permute-start | bytes 98312 | tf_op jit(solution)/shard_map/ppermute | solution.py:20
  674.3 6.8 copy.30
  681.1 187.6 %all-gather.11.cloned.1.call-done = bf16[1,4096,256]{2,1,0:T(8,128)(2,1)} async-done(((bf16[1,64,256]{2,1,0:T(8,128)(2,1)}), bf16[1,4096,256]{2,1,0:T(8,128)(2,1)}) %all-gather.11.cloned.1.call-update) | async-done | bytes 2097168 | tf_op jit(solution)/shard_map/all_gather | solution.py:34
  876.0 5.1 fusion.55
  884.6 6.8 copy.31
  891.4 5.1 fusion.56
  897.3 52.6 %collective-permute-start.14 = (bf16[1,64,256]{2,1,0:T(8,128)(2,1)S(1)}, bf16[1,64,256]{2,1,0:T(8,128)(2,1)S(1)}, u32[]{:S(2)}, u32[]{:S(2)}) collective-permute-start(bf16[1,64,256]{2,1,0:T(8,128)(2,1)S(1)} %copy-done.14), channel_id=1, source_target_pairs={{0,1},{1,2},{2,3},{4,5},{5,6},{6,7},{8,9},{9,10},{10,11},{12,13},{... | collective-permute-start | bytes 98312 | tf_op jit(solution)/shard_map/ppermute | solution.py:18
  951.9 4.7 collective-permute-done.15
  956.7 211.5 %all-gather.15.cloned.1.call-done = bf16[1,4096,256]{2,1,0:T(8,128)(2,1)} async-done(((bf16[1,64,256]{2,1,0:T(8,128)(2,1)}), bf16[1,4096,256]{2,1,0:T(8,128)(2,1)}) %all-gather.15.cloned.1.call-update) | async-done | bytes 2097168 | tf_op jit(solution)/shard_map/all_gather | solution.py:41
  1176.3 4.5 fusion.1
  1180.8 316.5 %all-reduce.5.cloned.1.call-done = (f32[3,3,256,256]{3,2,1,0:T(8,128)}, f32[3,3,256,256]{3,2,1,0:T(8,128)}) async-done(((f32[3,3,256,256]{3,2,1,0:T(8,128)}, f32[3,3,256,256]{3,2,1,0:T(8,128)}), (f32[3,3,256,256]{3,2,1,0:T(8,128)}, f32[3,3,256,256]{3,2,1,0:T(8,128)})) %all-reduce.5.cloned.1.call-update) | async-done | bytes 4718608 | tf_op jit(solution)/shard_map/psum | solution.py:137
  1497.3 5.1 broadcast_multiply_fusion
  (188 shorter events, 140.1 us)
Async XLA Ops:
  7.2 558.2 %copy-start = (bf16[3,3,256,256]{3,2,1,0:T(8,128)(2,1)S(1)}, bf16[3,3,256,256]{3,2,1,0:T(8,128)(2,1)}, u32[]{:S(2)}) copy-start(bf16[3,3,256,256]{3,2,1,0:T(8,128)(2,1)} %param.65) | copy-start | bytes 3538948
  7.2 251.8 %all-gather.9.cloned.1.call-start = ((), (), s32[]{:S(2)}) async-start(), calls=%async_computation | async-start | bytes 2129920 | tf_op jit(solution)/shard_map/all_gather | solution.py:34
  8.7 549.8 %all-gather.13.cloned.1.call-start = ((), (), s32[]{:S(2)}) async-start(), calls=%async_computation.2 | async-start | bytes 2129920 | tf_op jit(solution)/shard_map/all_gather | solution.py:41
  8.8 556.6 %copy-start.25 = (s32[256]{0:T(256)}, s32[256]{0:T(256)S(1)}, u32[]{:S(2)}) copy-start(s32[256]{0:T(256)S(1)} %and_select_fusion) | copy-start | bytes 3076
  70.5 4.1 collective-permute-start.8
  73.4 3.8 collective-permute-start.9
  83.2 785.5 %all-gather.11.cloned.1.call-start = ((), (), s32[]{:S(2)}) async-start(), calls=%async_computation.1 | async-start | bytes 2129920 | tf_op jit(solution)/shard_map/all_gather | solution.py:34
  83.2 178.4 %collective-permute-start = (bf16[1,64,256]{2,1,0:T(8,128)(2,1)S(1)}, bf16[1,64,256]{2,1,0:T(8,128)(2,1)S(1)}, u32[]{:S(2)}, u32[]{:S(2)}) collective-permute-start(bf16[1,64,256]{2,1,0:T(8,128)(2,1)S(1)} %copy-done.17), channel_id=1, source_target_pairs={{0,1},{1,2},{2,3},{4,5},{5,6},{6,7},{8,9},{9,10},{10,11},{12,13},{... | collective-permute-start | bytes 98312 | tf_op jit(solution)/shard_map/ppermute | solution.py:18
  90.1 171.5 %collective-permute-start.1 = (bf16[1,64,256]{2,1,0:T(8,128)(2,1)S(1)}, bf16[1,64,256]{2,1,0:T(8,128)(2,1)S(1)}, u32[]{:S(2)}, u32[]{:S(2)}) collective-permute-start(bf16[1,64,256]{2,1,0:T(8,128)(2,1)S(1)} %get-tuple-element.343), channel_id=1, source_target_pairs={{1,0},{2,1},{3,2},{5,4},{6,5},{7,6},{9,8},{10,9},{11,10},{13,12},{... | collective-permute-start | bytes 98312 | tf_op jit(solution)/shard_map/ppermute | solution.py:20
  92.8 472.5 %copy-start.22 = (pred[64]{0:T(512)(128)(4,1)}, pred[64]{0:T(512)(128)(4,1)S(1)}, u32[]{:S(2)}) copy-start(pred[64]{0:T(512)(128)(4,1)S(1)} %get-tuple-element.320) | copy-start | bytes 196
  94.1 172.1 %collective-permute-start.10 = (bf16[1,64,256]{2,1,0:T(8,128)(2,1)}, bf16[1,64,256]{2,1,0:T(8,128)(2,1)S(1)}, u32[]{:S(2)}, u32[]{:S(2)}) collective-permute-start(bf16[1,64,256]{2,1,0:T(8,128)(2,1)} %get-tuple-element.324), channel_id=1, source_target_pairs={{0,1},{1,2},{2,3},{4,5},{5,6},{6,7},{8,9},{9,10},{10,11},{12,13},{... | collective-permute-start | bytes 98312 | tf_op jit(solution)/shard_map/ppermute | solution.py:18
  99.3 167.0 %collective-permute-start.11 = (bf16[1,64,256]{2,1,0:T(8,128)(2,1)S(1)}, bf16[1,64,256]{2,1,0:T(8,128)(2,1)S(1)}, u32[]{:S(2)}, u32[]{:S(2)}) collective-permute-start(bf16[1,64,256]{2,1,0:T(8,128)(2,1)S(1)} %get-tuple-element.325), channel_id=1, source_target_pairs={{1,0},{2,1},{3,2},{5,4},{6,5},{7,6},{9,8},{10,9},{11,10},{13,12},{... | collective-permute-start | bytes 98312 | tf_op jit(solution)/shard_map/ppermute | solution.py:20
  261.7 5.7 collective-permute-start.2
  262.9 4.4 collective-permute-start.3
  571.2 596.9 %all-gather.15.cloned.1.call-start = ((), (), s32[]{:S(2)}) async-start(), calls=%async_computation.3 | async-start | bytes 2129920 | tf_op jit(solution)/shard_map/all_gather | solution.py:41
  609.3 5.5 collective-permute-start.12
  610.6 4.2 collective-permute-start.13
  619.1 878.2 %all-reduce.5.cloned.1.call-start = ((), (), s32[]{:S(2)}) async-start(), calls=%async_computation.4 | async-start | bytes 9437184 | tf_op jit(solution)/shard_map/psum | solution.py:137
  619.2 252.2 %collective-permute-start.5 = (bf16[1,64,256]{2,1,0:T(8,128)(2,1)}, bf16[1,64,256]{2,1,0:T(8,128)(2,1)S(1)}, u32[]{:S(2)}, u32[]{:S(2)}) collective-permute-start(bf16[1,64,256]{2,1,0:T(8,128)(2,1)} %get-tuple-element.341), channel_id=1, source_target_pairs={{1,0},{2,1},{3,2},{5,4},{6,5},{7,6},{9,8},{10,9},{11,10},{13,12},{... | collective-permute-start | bytes 98312 | tf_op jit(solution)/shard_map/ppermute | solution.py:20
  670.0 201.4 %collective-permute-start.4 = (bf16[1,64,256]{2,1,0:T(8,128)(2,1)}, bf16[1,64,256]{2,1,0:T(8,128)(2,1)S(1)}, u32[]{:S(2)}, u32[]{:S(2)}) collective-permute-start(bf16[1,64,256]{2,1,0:T(8,128)(2,1)} %get-tuple-element.340), channel_id=1, source_target_pairs={{0,1},{1,2},{2,3},{4,5},{5,6},{6,7},{8,9},{9,10},{10,11},{12,13},{... | collective-permute-start | bytes 98312 | tf_op jit(solution)/shard_map/ppermute | solution.py:18
  871.5 9.7 collective-permute-start.6
  873.5 7.7 collective-permute-start.7
  897.3 54.6 %collective-permute-start.14 = (bf16[1,64,256]{2,1,0:T(8,128)(2,1)S(1)}, bf16[1,64,256]{2,1,0:T(8,128)(2,1)S(1)}, u32[]{:S(2)}, u32[]{:S(2)}) collective-permute-start(bf16[1,64,256]{2,1,0:T(8,128)(2,1)S(1)} %copy-done.14), channel_id=1, source_target_pairs={{0,1},{1,2},{2,3},{4,5},{5,6},{6,7},{8,9},{9,10},{10,11},{12,13},{... | collective-permute-start | bytes 98312 | tf_op jit(solution)/shard_map/ppermute | solution.py:18
  949.9 6.7 collective-permute-start.15
  (27 other events, 2656.5 us)
Sparse Core Ops, SparseCore 0:
  10.4 248.6 all-gather.8
  261.4 297.1 all-gather.12
  571.4 297.2 all-gather.10
  870.3 297.7 all-gather.14
  1174.2 323.0 all-reduce.4
where the time goes:
time: 1510 us
  waiting for transfers between devices  1160 us (77%)
  starting transfers between devices  142 us (9%)
  local copies, waits for them, and re-layouts  106 us (7%)
  other arithmetic  56.4 us (4%)
  matrix products  25.3 us (2%)
    all_gather x2, waiting for transfers between devices, fold_backward(): lax.all_gather(fold_grad.astype(jnp.bfloat16), 'zonal', axis=0, tiled=True)  494 us
    all_gather x2, waiting for transfers between devices, fold_forward(): whole_row = lax.all_gather(top_row, 'zonal', axis=0, tiled=True)  345 us
    psum x1, waiting for transfers between devices, shards(): grad_one, grad_two = lax.psum((grad_one, grad_two), ('zonal', 'merid'))  317 us
    ppermute x8, starting transfers between devices, with_halo(): lax.ppermute(tail, axis, [(i, (i + 1) % count) for i in range(ends)])  76.3 us
    ppermute x8, starting transfers between devices, with_halo(): lax.ppermute(head, axis, [((i + 1) % count, i) for i in range(ends)])  65.5 us
    scatter-add x14, local copies, waits for them, and re-layouts, transpose_conv(): grad_pad.at[row_step:row_step + rows, col_step:col_step + columns]  51.2 us
  transfers between devices with their start and end apart: 21, of which 9 were waited for; matrix products, arithmetic and copies ran while one was open for 10% of the time, Pallas kernels for 0%

commit v1 on v0

--- a/solution.py
+++ b/solution.py
@@ -1,10 +1,21 @@
+import functools
 import math
 import jax
 import jax.numpy as jnp
 from jax import lax
 from jax.sharding import PartitionSpec as P
+from jax.lax import psum
 
 LEV = 64
+
+
+def feed_leaves_over_axis(mat, mesh_ax, row_axis):
+    for at in (mesh_ax, row_axis):
+        mat = psum(mat, axis_name=at)
+    return mat
+
+
+feed_fields = functools.partial(feed_leaves_over_axis, mesh_ax="zonal", row_axis="merid")
 
 
 def with_halo(cells, sides, width, closed):
@@ -134,7 +145,7 @@
         transpose_conv(delta_one, flat_one, rows, columns), fold_partner, is_top
     )
     input_grad = (masked_grad + field_grad).astype(jnp.bfloat16)
-    grad_one, grad_two = lax.psum((grad_one, grad_two), ("zonal", "merid"))
+    grad_one, grad_two = feed_fields((grad_one, grad_two))
     scale = 1.0 / math.sqrt(rows * columns * lax.axis_size("zonal") * lax.axis_size("merid"))
     return (output, input_grad, grad_one * scale, grad_two * scale)
 

time: 1510 us -> 1990 us (1.32)
  waiting for transfers between devices: 1160 us -> 1620 us
  local copies, waits for them, and re-layouts: 106 us -> 128 us
    psum x1 -> x2, waiting for transfers between devices: 317 us -> 698 us  [feed_leaves_over_axis(): mat = psum(mat, axis_name=at)]
    all_gather x2, waiting for transfers between devices: 345 us -> 393 us  [fold_forward(): whole_row = lax.all_gather(top_row, 'zonal', axis=0, tiled=True)]
    all_gather x2, waiting for transfers between devices: 494 us -> 521 us  [fold_backward(): lax.all_gather(fold_grad.astype(jnp.bfloat16), 'zonal', axis=0, tiled=True)]
  transfers between devices with their start and end apart: 21 -> 22, of which waited for: 9 -> 10; matrix products, arithmetic and copies ran while one was open for 10% -> 9% of each run, Pallas kernels for 0% -> 0%
where the time goes in v1:
time: 1990 us
  waiting for transfers between devices  1620 us (81%)
  starting transfers between devices  138 us (7%)
  local copies, waits for them, and re-layouts  128 us (6%)
  other arithmetic  65.2 us (3%)
  matrix products  23.6 us (1%)
    psum x2, waiting for transfers between devices, feed_leaves_over_axis(): mat = psum(mat, axis_name=at)  698 us
    all_gather x2, waiting for transfers between devices, fold_backward(): lax.all_gather(fold_grad.astype(jnp.bfloat16), 'zonal', axis=0, tiled=True)  521 us
    all_gather x2, waiting for transfers between devices, fold_forward(): whole_row = lax.all_gather(top_row, 'zonal', axis=0, tiled=True)  393 us
    ppermute x8, starting transfers between devices, with_halo(): lax.ppermute(tail, axis, [(i, (i + 1) % count) for i in range(ends)])  74.2 us
    scatter-add x14, local copies, waits for them, and re-layouts, transpose_conv(): grad_pad.at[row_step:row_step + rows, col_step:col_step + columns]  67 us
    ppermute x8, starting transfers between devices, with_halo(): lax.ppermute(head, axis, [((i + 1) % count, i) for i in range(ends)])  63.3 us
  transfers between devices with their start and end apart: 22, of which 10 were waited for; matrix products, arithmetic and copies ran while one was open for 9% of the time, Pallas kernels for 0%

profile of v1, /device:TPU:97, one launch (start us, length us, event | category | flops | bytes accessed | tf_op | source)
XLA Modules:
  0.0 1988.9 jit_solution(3852257070031251452)
XLA Ops:
  18.9 6.4 scatter-add.89
  31.1 6.5 scatter-add.90
  41.4 5.1 scatter-add.94
  48.9 5.1 scatter-add.95
  57.8 5.1 scatter-add.99
  65.3 5.1 scatter-add.100
  84.6 6.8 collective-permute-start
  95.5 5.1 collective-permute-start.10
  102.5 156.5 %all-gather.9.cloned.1.call-done = bf16[1,4096,256]{2,1,0:T(8,128)(2,1)} async-done(((bf16[1,64,256]{2,1,0:T(8,128)(2,1)}), bf16[1,4096,256]{2,1,0:T(8,128)(2,1)}) %all-gather.9.cloned.1.call-update) | async-done | bytes 2097168 | tf_op jit(solution)/shard_map/all_gather | solution.py:45
  276.3 282.2 %all-gather.13.cloned.1.call-done = bf16[1,4096,256]{2,1,0:T(8,128)(2,1)} async-done(((bf16[1,64,256]{2,1,0:T(8,128)(2,1)}), bf16[1,4096,256]{2,1,0:T(8,128)(2,1)}) %all-gather.13.cloned.1.call-update) | async-done | bytes 2097168 | tf_op jit(solution)/shard_map/all_gather | solution.py:52
  571.7 49.7 %collective-permute-start.5 = (bf16[1,64,256]{2,1,0:T(8,128)(2,1)S(1)}, bf16[1,64,256]{2,1,0:T(8,128)(2,1)S(1)}, u32[]{:S(2)}, u32[]{:S(2)}) collective-permute-start(bf16[1,64,256]{2,1,0:T(8,128)(2,1)S(1)} %get-tuple-element.343), channel_id=1, source_target_pairs={{1,0},{2,1},{3,2},{5,4},{6,5},{7,6},{9,8},{10,9},{11,10},{13,12},{... | collective-permute-start | bytes 98312 | tf_op jit(solution)/shard_map/ppermute | solution.py:31
  625.7 6.7 copy.30
  632.3 236.7 %all-gather.11.cloned.1.call-done = bf16[1,4096,256]{2,1,0:T(8,128)(2,1)} async-done(((bf16[1,64,256]{2,1,0:T(8,128)(2,1)}), bf16[1,4096,256]{2,1,0:T(8,128)(2,1)}) %all-gather.11.cloned.1.call-update) | async-done | bytes 2097168 | tf_op jit(solution)/shard_map/all_gather | solution.py:45
  876.1 5.1 fusion.55
  884.7 6.7 copy.31
  891.4 5.1 fusion.56
  904.3 6.4 scatter-add.110
  915.1 6.5 scatter-add.111
  925.4 5.1 scatter-add.115
  932.9 5.1 scatter-add.116
  964.6 553.4 %all-reduce.7.cloned.1.call-done = (f32[3,3,256,256]{3,2,1,0:T(8,128)}, f32[3,3,256,256]{3,2,1,0:T(8,128)}) async-done(((f32[3,3,256,256]{3,2,1,0:T(8,128)}, f32[3,3,256,256]{3,2,1,0:T(8,128)}), (f32[3,3,256,256]{3,2,1,0:T(8,128)}, f32[3,3,256,256]{3,2,1,0:T(8,128)})) %all-reduce.7.cloned.1.call-update) | async-done | bytes 4718608 | tf_op jit(solution)/shard_map/psum | solution.py:14
  1518.8 52.4 %collective-permute-start.14 = (bf16[1,64,256]{2,1,0:T(8,128)(2,1)S(1)}, bf16[1,64,256]{2,1,0:T(8,128)(2,1)S(1)}, u32[]{:S(2)}, u32[]{:S(2)}) collective-permute-start(bf16[1,64,256]{2,1,0:T(8,128)(2,1)S(1)} %copy-done.10), channel_id=1, source_target_pairs={{0,1},{1,2},{2,3},{4,5},{5,6},{6,7},{8,9},{9,10},{10,11},{12,13},{... | collective-permute-start | bytes 98312 | tf_op jit(solution)/shard_map/ppermute | solution.py:29
  1578.6 238.5 %all-gather.15.cloned.1.call-done = bf16[1,4096,256]{2,1,0:T(8,128)(2,1)} async-done(((bf16[1,64,256]{2,1,0:T(8,128)(2,1)}), bf16[1,4096,256]{2,1,0:T(8,128)(2,1)}) %all-gather.15.cloned.1.call-update) | async-done | bytes 2097168 | tf_op jit(solution)/shard_map/all_gather | solution.py:52
  1832.5 144.6 %all-reduce.9.cloned.1.call-done = (f32[3,3,256,256]{3,2,1,0:T(8,128)}, f32[3,3,256,256]{3,2,1,0:T(8,128)}) async-done(((f32[3,3,256,256]{3,2,1,0:T(8,128)}, f32[3,3,256,256]{3,2,1,0:T(8,128)}), (f32[3,3,256,256]{3,2,1,0:T(8,128)}, f32[3,3,256,256]{3,2,1,0:T(8,128)})) %all-reduce.9.cloned.1.call-update) | async-done | bytes 4718608 | tf_op jit(solution)/shard_map/psum | solution.py:14
  (187 shorter events, 168.1 us)
Async XLA Ops:
  7.2 251.8 %all-gather.9.cloned.1.call-start = ((), (), s32[]{:S(2)}) async-start(), calls=%async_computation | async-start | bytes 2129920 | tf_op jit(solution)/shard_map/all_gather | solution.py:45
  8.7 549.8 %all-gather.13.cloned.1.call-start = ((), (), s32[]{:S(2)}) async-start(), calls=%async_computation.2 | async-start | bytes 2129920 | tf_op jit(solution)/shard_map/all_gather | solution.py:52
  70.6 4.1 collective-permute-start.8
  73.5 3.8 collective-permute-start.9
  84.5 784.5 %all-gather.11.cloned.1.call-start = ((), (), s32[]{:S(2)}) async-start(), calls=%async_computation.1 | async-start | bytes 2129920 | tf_op jit(solution)/shard_map/all_gather | solution.py:45
  84.6 177.1 %collective-permute-start = (bf16[1,64,256]{2,1,0:T(8,128)(2,1)}, bf16[1,64,256]{2,1,0:T(8,128)(2,1)S(1)}, u32[]{:S(2)}, u32[]{:S(2)}) collective-permute-start(bf16[1,64,256]{2,1,0:T(8,128)(2,1)} %get-tuple-element.344), channel_id=1, source_target_pairs={{0,1},{1,2},{2,3},{4,5},{5,6},{6,7},{8,9},{9,10},{10,11},{12,13},{... | collective-permute-start | bytes 98312 | tf_op jit(solution)/shard_map/ppermute | solution.py:29
  91.4 170.1 %collective-permute-start.1 = (bf16[1,64,256]{2,1,0:T(8,128)(2,1)}, bf16[1,64,256]{2,1,0:T(8,128)(2,1)S(1)}, u32[]{:S(2)}, u32[]{:S(2)}) collective-permute-start(bf16[1,64,256]{2,1,0:T(8,128)(2,1)} %get-tuple-element.345), channel_id=1, source_target_pairs={{1,0},{2,1},{3,2},{5,4},{6,5},{7,6},{9,8},{10,9},{11,10},{13,12},{... | collective-permute-start | bytes 98312 | tf_op jit(solution)/shard_map/ppermute | solution.py:31
  94.1 777.4 %copy-start.19 = (pred[64]{0:T(512)(128)(4,1)}, pred[64]{0:T(512)(128)(4,1)S(1)}, u32[]{:S(2)}) copy-start(pred[64]{0:T(512)(128)(4,1)S(1)} %get-tuple-element.322) | copy-start | bytes 196
  94.1 774.9 %copy-start.21 = (s32[1024]{0:T(1024)}, s32[1024]{0:T(1024)S(1)}, u32[]{:S(2)}) copy-start(s32[1024]{0:T(1024)S(1)} %pad_clamp_fusion) | copy-start | bytes 12292
  95.5 170.8 %collective-permute-start.10 = (bf16[1,64,256]{2,1,0:T(8,128)(2,1)}, bf16[1,64,256]{2,1,0:T(8,128)(2,1)S(1)}, u32[]{:S(2)}, u32[]{:S(2)}) collective-permute-start(bf16[1,64,256]{2,1,0:T(8,128)(2,1)} %get-tuple-element.326), channel_id=1, source_target_pairs={{0,1},{1,2},{2,3},{4,5},{5,6},{6,7},{8,9},{9,10},{10,11},{12,13},{... | collective-permute-start | bytes 98312 | tf_op jit(solution)/shard_map/ppermute | solution.py:29
  100.6 165.7 %collective-permute-start.11 = (bf16[1,64,256]{2,1,0:T(8,128)(2,1)S(1)}, bf16[1,64,256]{2,1,0:T(8,128)(2,1)S(1)}, u32[]{:S(2)}, u32[]{:S(2)}) collective-permute-start(bf16[1,64,256]{2,1,0:T(8,128)(2,1)S(1)} %get-tuple-element.327), channel_id=1, source_target_pairs={{1,0},{2,1},{3,2},{5,4},{6,5},{7,6},{9,8},{10,9},{11,10},{13,12},{... | collective-permute-start | bytes 98312 | tf_op jit(solution)/shard_map/ppermute | solution.py:31
  261.7 5.7 collective-permute-start.2
  263.0 4.4 collective-permute-start.3
  571.7 946.4 %all-reduce.7.cloned.1.call-start = ((), (), s32[]{:S(2)}) async-start(), calls=%async_computation.4 | async-start | bytes 9437184 | tf_op jit(solution)/shard_map/psum | solution.py:14
  571.7 299.8 %collective-permute-start.5 = (bf16[1,64,256]{2,1,0:T(8,128)(2,1)S(1)}, bf16[1,64,256]{2,1,0:T(8,128)(2,1)S(1)}, u32[]{:S(2)}, u32[]{:S(2)}) collective-permute-start(bf16[1,64,256]{2,1,0:T(8,128)(2,1)S(1)} %get-tuple-element.343), channel_id=1, source_target_pairs={{1,0},{2,1},{3,2},{5,4},{6,5},{7,6},{9,8},{10,9},{11,10},{13,12},{... | collective-permute-start | bytes 98312 | tf_op jit(solution)/shard_map/ppermute | solution.py:31
  621.4 250.2 %collective-permute-start.4 = (bf16[1,64,256]{2,1,0:T(8,128)(2,1)}, bf16[1,64,256]{2,1,0:T(8,128)(2,1)S(1)}, u32[]{:S(2)}, u32[]{:S(2)}) collective-permute-start(bf16[1,64,256]{2,1,0:T(8,128)(2,1)} %get-tuple-element.342), channel_id=1, source_target_pairs={{0,1},{1,2},{2,3},{4,5},{5,6},{6,7},{8,9},{9,10},{10,11},{12,13},{... | collective-permute-start | bytes 98312 | tf_op jit(solution)/shard_map/ppermute | solution.py:29
  871.7 9.5 collective-permute-start.6
  873.0 8.3 collective-permute-start.7
  896.5 920.6 %all-gather.15.cloned.1.call-start = ((), (), s32[]{:S(2)}) async-start(), calls=%async_computation.3 | async-start | bytes 2129920 | tf_op jit(solution)/shard_map/all_gather | solution.py:52
  954.6 2.7 collective-permute-start.12
  954.7 3.9 collective-permute-start.13
  964.6 1012.5 %all-reduce.9.cloned.1.call-start = ((), (), s32[]{:S(2)}) async-start(), calls=%async_computation.5 | async-start | bytes 9437184 | tf_op jit(solution)/shard_map/psum | solution.py:14
  1518.8 55.4 %collective-permute-start.14 = (bf16[1,64,256]{2,1,0:T(8,128)(2,1)S(1)}, bf16[1,64,256]{2,1,0:T(8,128)(2,1)S(1)}, u32[]{:S(2)}, u32[]{:S(2)}) collective-permute-start(bf16[1,64,256]{2,1,0:T(8,128)(2,1)S(1)} %copy-done.10), channel_id=1, source_target_pairs={{0,1},{1,2},{2,3},{4,5},{5,6},{6,7},{8,9},{9,10},{10,11},{12,13},{... | collective-permute-start | bytes 98312 | tf_op jit(solution)/shard_map/ppermute | solution.py:29
  1571.2 6.7 collective-permute-start.15
  (26 other events, 3375.5 us)
Sparse Core Ops, SparseCore 0:
  10.3 248.6 all-gather.8
  261.4 297.1 all-gather.12
  571.8 297.1 all-gather.10
  896.7 621.3 all-reduce.6
  1520.3 296.7 all-gather.14
  1819.7 157.3 all-reduce.8
